TPU v7x, 512 devices: a whole 4x8x8 slice. The times are simulated.
512 devices in a mesh: fsdp: 16 (over y, x_lo), ed: 32 (over x_hi, z, core).
Axes of the slice: x: 4 (x_hi: 2, x_lo: 2; x = x_hi * 2 + x_lo), y: 8, z: 8, core: 2. Of those that a mesh axis runs over, the one named last changes fastest.
Arguments:
- tokens: bfloat16 [9216, 6144], P('ed', 'fsdp'), may hold values from -6 to 6
- expert_ids: int32 [9216, 2], P('ed'), may hold values from 0 to 7, all different within a row; in each aligned block of 288 rows (0 to 287, 288 to 575, ...) at most 81 rows name the same one
- route_weights: float32 [9216, 2], P('ed'), may hold values from 0.1 to 1
- w_gate: bfloat16 [1, 6144, 8192], P(None, 'fsdp', 'ed'), may hold values from -0.078125 to 0.078125
- w_up: bfloat16 [1, 6144, 8192], P(None, 'fsdp', 'ed'), may hold values from -0.078125 to 0.078125
- w_down: bfloat16 [1, 8192, 6144], P(None, 'ed', 'fsdp'), may hold values from -0.0625 to 0.0625
Outputs:
- mixed: bfloat16 [9216, 6144], P('ed', 'fsdp')
Inputs may be any that keep to these rules, and one draw needn't show every extreme that they name: `expert_ids`: each row names two different experts. In each block of 288 rows that one index of ed holds, no expert is named by more than 81 rows, a bound that some block reaches.
All inputs are finite; a program needn't handle non-finite values.
Results may differ from a plain program's by a relative error of at most 0.025.
Values may be sent and summed in bfloat16 or wider, within the bound.
A program may use at most 64 MiB of HBM per device.

v0:
```python
import jax
import jax.numpy as jnp
from jax import lax
from jax.sharding import PartitionSpec as P

CAP = 81


def slot_match(routes, window, capacity):
    window_ids = jnp.arange(window, dtype=jnp.int32)
    routed = jnp.any(routes[:, :, None, :] == window_ids[None, None, :, None], axis=3)
    position = jnp.cumsum(routed.astype(jnp.int32), axis=1) - 1
    slot_ids = jnp.arange(capacity, dtype=jnp.int32)
    hits = routed[:, :, :, None] & (position[:, :, :, None] == slot_ids[None, None, None, :])
    return hits.astype(jnp.int32)


def take_block(block_rows, row_list):
    return jnp.take(block_rows, row_list, axis=0)


def pick_rows(blocks, routes, window, capacity):
    match = slot_match(routes, window, capacity)
    row_numbers = jnp.arange(blocks.shape[1], dtype=jnp.int32)
    source_row = jnp.sum(match * row_numbers[None, :, None, None], axis=1).reshape(
        blocks.shape[0], window * capacity
    )
    filled = jnp.sum(match, axis=1).reshape(blocks.shape[0], window * capacity)
    picked = jax.vmap(take_block)(blocks, source_row)
    picked = jnp.where(filled[:, :, None] > 0, picked, jnp.zeros_like(picked))
    return picked.reshape(blocks.shape[0], window, capacity, blocks.shape[2])


def combine_matrix(routes, weights, window, capacity):
    match = slot_match(routes[None], window, capacity)[0]
    window_ids = jnp.arange(window, dtype=jnp.int32)
    per_expert = jnp.sum(
        jnp.where(
            routes[:, None, :] == window_ids[None, :, None],
            weights[:, None, :],
            jnp.zeros_like(weights[:, None, :]),
        ),
        axis=2,
    )
    return (per_expert[:, :, None] * match.astype(weights.dtype)).reshape(
        routes.shape[0], window * capacity
    )


def local(tokens, expert_ids, route_weights, w_gate, w_up, w_down):
    window = w_gate.shape[0]
    features_dev = tokens.shape[1]
    own_slots = pick_rows(tokens[None], expert_ids[None], window, CAP)[0]
    selected = lax.all_gather(own_slots, "ed", axis=1, tiled=True)
    rows_full = lax.all_to_all(selected, "fsdp", split_axis=1, concat_axis=2, tiled=True)
    gate_part = jnp.einsum(
        "hnm,hmq->hnq",
        rows_full,
        lax.all_gather(w_gate, "fsdp", axis=1, tiled=True),
        preferred_element_type=jnp.float32,
    )
    up_part = jnp.einsum(
        "hnm,hmq->hnq",
        rows_full,
        lax.all_gather(w_up, "fsdp", axis=1, tiled=True),
        preferred_element_type=jnp.float32,
    )
    activation = (jax.nn.silu(gate_part) * up_part).astype(jnp.bfloat16)
    act_one = activation[0]

    def columns_out(shard_piece, first_col, act_one=act_one):
        return jnp.dot(act_one, shard_piece, preferred_element_type=jnp.float32)

    whole_rows = columns_out(lax.all_gather(w_down[0], "fsdp", axis=1, tiled=True), jnp.int32(0))
    outputs_list = [whole_rows.astype(jnp.bfloat16)]
    stacked = jnp.stack(outputs_list)
    exchanged = lax.all_to_all(stacked, "fsdp", split_axis=2, concat_axis=1, tiled=True)
    partial_out = exchanged.astype(jnp.float32)
    slot_out = lax.psum_scatter(
        partial_out.astype(jnp.bfloat16), "ed", scatter_dimension=1, tiled=True
    ).astype(jnp.float32)
    weights_matrix = combine_matrix(expert_ids, route_weights, window, CAP)
    mixed = jnp.dot(
        weights_matrix,
        slot_out.reshape(window * CAP, features_dev),
        precision=lax.Precision.HIGHEST,
        preferred_element_type=jnp.float32,
    )
    return mixed.astype(jnp.bfloat16)


def solution(mesh):
    return jax.shard_map(
        local,
        mesh=mesh,
        in_specs=(
            P("ed", "fsdp"),
            P("ed", None),
            P("ed", None),
            P(None, "fsdp", "ed"),
            P(None, "fsdp", "ed"),
            P(None, "ed", "fsdp"),
        ),
        out_specs=P("ed", "fsdp"),
        check_vma=False,
    )
```

profile of v0, /device:TPU:1, one launch (start us, length us, event | category | flops | bytes accessed | tf_op | source)
XLA Modules:
  0.0 640.9 jit_solution(6663339600788899471)
XLA Ops:
  6.5 0.0 copy-start
  6.5 0.0 all-gather.6.cloned.1.call-start
  6.5 0.7 fusion.27
  7.3 0.3 reduce-window.6
  7.6 0.2 slice_reduce_fusion
  7.8 0.2 reduce-window.9
  8.0 0.1 broadcast.258
  8.1 3.0 convert_reduce_fusion
  11.1 0.0 copy-done
  11.1 1.3 gather_fusion
  12.4 0.1 fusion.22
  12.5 0.7 copy.18
  13.3 0.0 all-gather.6.cloned.1.call-update
  13.3 0.0 all-gather.8.cloned.1.call-start
  13.4 0.7 all-gather.8.cloned.1.call-update
  14.1 0.0 all-gather.10.cloned.1.call-start
  14.1 0.7 all-gather.10.cloned.1.call-update
  14.8 0.0 all-gather.12.cloned.1.call-start
  14.8 0.5 all-gather.12.cloned.1.call-update
  15.4 96.3 %all-gather.6.cloned.1.call-done = bf16[1,2592,384]{2,0,1:T(2,128)(2,1)} async-done(((bf16[1,81,384]{2,0,1:T(2,128)(2,1)}), bf16[1,2592,384]{2,0,1:T(2,128)(2,1)}) %all-gather.6.cloned.1.call-update) | async-done | bytes 1990672 | tf_op jit(solution)/shard_map/all_gather | solution.py:54
  111.6 0.5 broadcast.283
  112.2 15.8 %reduce.14 = bf16[2592,384]{1,0:T(8,128)(2,1)S(1)} reduce(bf16[2592,1,384]{2,1,0:T(2,128)(2,1)} %bitcast.80, bf16[]{:T(256)} %broadcast.283), dimensions={1}, to_apply=%bitcast.61.reduce_sub_computation | reduce | bytes 3981314
  128.0 1.6 reshape.463
  129.6 71.7 %all_to_all.33 = bf16[16,2,31104]{2,1,0:T(2,128)(2,1)S(1)} all-to-all(bf16[16,2,31104]{2,1,0:T(2,128)(2,1)} %reshape.463), channel_id=1, replica_groups=mesh['fsdp'=16,'ed'=32] {'fsdp'}, dimensions={0} | all-to-all | bytes 3981312 | tf_op jit(solution)/shard_map/all_to_all | solution.py:55
  201.2 8.9 %reshape.464 = bf16[2592,1,384]{2,1,0:T(2,128)(2,1)} reshape(bf16[16,2,31104]{2,1,0:T(2,128)(2,1)S(1)} %all_to_all.33) | data formatting | bytes 3981312
  210.2 17.6 %bitcast_reduce_fusion = bf16[2592,384]{1,0:T(8,128)(2,1)} fusion(bf16[2592,1,384]{2,1,0:T(2,128)(2,1)} %reshape.464), kind=kLoop, calls=%fused_computation.46 | loop fusion | bytes 3981312 | tf_op jit(solution)/shard_map/all_to_all | solution.py:55
  227.8 1.8 all_to_all.25
  229.5 0.3 copy.29
  229.8 0.2 pad.7
  230.0 0.5 copy.26
  230.6 0.0 all-gather.8.cloned.1.call-done
  230.6 2.7 fusion.5
  233.3 66.1 %all-gather.10.cloned.1.call-done = bf16[1,6144,256]{2,1,0:T(8,128)(2,1)} async-done(((bf16[1,384,256]{2,1,0:T(8,128)(2,1)}), bf16[1,6144,256]{2,1,0:T(8,128)(2,1)}) %all-gather.10.cloned.1.call-update) | async-done | bytes 3145744 | tf_op jit(solution)/shard_map/all_gather | solution.py:65
  299.3 85.3 %all-gather.12.cloned.1.call-done = bf16[1,256,6144]{2,1,0:T(8,128)(2,1)} async-done(((bf16[1,256,384]{2,1,0:T(8,128)(2,1)}), bf16[1,256,6144]{2,1,0:T(8,128)(2,1)}) %all-gather.12.cloned.1.call-update) | async-done | bytes 3145744 | tf_op jit(solution)/shard_map/all_gather | solution.py:74
  384.6 6.5 %fusion.1 = bf16[1,162,6144]{2,1,0:T(8,128)(2,1)} fusion(bf16[1,256,6144]{2,1,0:T(8,128)(2,1)} %all-gather.12.cloned.1.call-done, bf16[162,6144]{1,0:T(8,128)(2,1)S(1)} %bitcast.74, bf16[1,6144,256]{2,1,0:T(8,128)(2,1)} %all-gather.10.cloned.1.call-done, f32[162,256]{1,0:T(8,128)S(1)} %fusion.5), kind=kOutput, calls=%fused_computation.2 | convolution fusion | flops 1020460032 | bytes 10438656 | tf_op jit(solution)/shard_map/dot_general | solution.py:72
  391.1 13.7 %copy.20 = bf16[1,162,6144]{1,0,2:T(2,128)(2,1)} copy(bf16[1,162,6144]{2,1,0:T(8,128)(2,1)} %fusion.1) | data formatting | bytes 3981312 | tf_op jit(solution)/shard_map/stack | solution.py:76
  404.8 34.6 %reduce.15 = bf16[6144,162]{1,0:T(8,128)(2,1)S(1)} reduce(bf16[6144,1,162]{2,1,0:T(2,128)(2,1)} %bitcast.71, bf16[]{:T(256)} %broadcast.283), dimensions={1}, to_apply=%bitcast.63.reduce_sub_computation | reduce | bytes 3981314
  439.4 6.9 %reshape.465 = bf16[16,2,31104]{2,1,0:T(2,128)(2,1)} reshape(bf16[6144,162]{1,0:T(8,128)(2,1)S(1)} %reduce.15) | data formatting | bytes 3981312
  446.4 4.2 all-to-all-start.1
  450.6 0.0 copy-done.2
  450.6 0.0 copy-done.3
  450.7 42.9 %all-to-all-done.1 = bf16[16,2,31104]{2,1,0:T(2,128)(2,1)S(1)} async-done(((bf16[16,2,31104]{2,1,0:T(2,128)(2,1)}), bf16[16,2,31104]{2,1,0:T(2,128)(2,1)S(1)}, u32[]{:S(2)}, u32[]{:S(2)}) %all-to-all-start.1) | async-done | bytes 1990688 | tf_op jit(solution)/shard_map/all_to_all | solution.py:77
  493.5 12.1 %reshape.466 = bf16[6144,1,162]{2,1,0:T(2,128)(2,1)} reshape(bf16[16,2,31104]{2,1,0:T(2,128)(2,1)S(1)} %all-to-all-done.1) | data formatting | bytes 3981312
  505.6 13.8 %copy.21 = bf16[1,162,6144]{2,1,0:T(8,128)(2,1)S(1)} copy(bf16[1,162,6144]{1,0,2:T(2,128)(2,1)} %bitcast.72) | data formatting | bytes 3981312 | tf_op jit(solution)/shard_map/all_to_all | solution.py:77
  519.4 0.4 copy.27
  519.8 0.2 bitcast_bitcast_fusion
  520.0 0.4 copy.22
  520.5 0.0 copy-start.1
  520.5 1.6 all_to_all.30
  522.0 81.8 %fusion = bf16[96,384]{1,0:T(8,128)(2,1)S(1)} fusion(bf16[1,2592,384]{2,1,0:T(8,128)(2,1)} %all_to_all.30), kind=kCustom, calls=%all-reduce-scatter | all-reduce-scatter fusion | flops 1179649 | bytes 2066432
  603.9 3.5 collective-permute-start
  607.5 1.3 collective-permute-start.1
  608.8 1.3 collective-permute-start.2
  610.1 1.3 collective-permute-start.3
  611.4 16.7 %collective-permute-start.4 = (bf16[81,384]{1,0:T(8,128)(2,1)S(1)}, bf16[81,384]{1,0:T(8,128)(2,1)S(1)}, u32[]{:S(2)}, u32[]{:S(2)}) collective-permute-start(bf16[81,384]{1,0:T(8,128)(2,1)S(1)} %slice.16), channel_id=1, source_target_pairs={{0,5},{1,6},{2,7},{3,8},{4,9},{5,10},{6,11},{7,12},{8,13},{9,14},{... | collective-permute-start | bytes 186632
  628.1 1.7 convert_multiply_fusion
  629.8 1.3 dynamic-slice.4
  631.7 0.0 collective-permute-done.4
  631.7 0.0 collective-permute-done
  631.7 0.0 collective-permute-done.1
  631.7 0.0 collective-permute-done.2
  631.7 0.0 collective-permute-done.3
  631.8 1.6 concatenate.3
  633.4 1.0 convolution_convert_fusion.1
  (15 shorter events, 0.2 us)
Async XLA Ops:
  6.5 4.6 copy-start
  6.5 105.1 %all-gather.6.cloned.1.call-start = ((), (), s32[]{:S(2)}) async-start(), calls=%async_computation.2 | async-start | bytes 4105728 | tf_op jit(solution)/shard_map/all_gather | solution.py:54
  13.3 217.3 %all-gather.8.cloned.1.call-start = ((), (), s32[]{:S(2)}) async-start(), calls=%async_computation.3 | async-start | bytes 3342336 | tf_op jit(solution)/shard_map/all_gather | solution.py:59
  14.1 285.3 %all-gather.10.cloned.1.call-start = ((), (), s32[]{:S(2)}) async-start(), calls=%async_computation.4 | async-start | bytes 3342336 | tf_op jit(solution)/shard_map/all_gather | solution.py:65
  14.8 369.8 %all-gather.12.cloned.1.call-start = ((), (), s32[]{:S(2)}) async-start(), calls=%async_computation.5 | async-start | bytes 3342336 | tf_op jit(solution)/shard_map/all_gather | solution.py:74
  446.4 4.2 copy-start.2
  446.4 4.3 copy-start.3
  446.4 47.1 %all-to-all-start.1 = ((bf16[16,2,31104]{2,1,0:T(2,128)(2,1)}), bf16[16,2,31104]{2,1,0:T(2,128)(2,1)S(1)}, u32[]{:S(2)}, u32[]{:S(2)}) async-start(bf16[16,2,31104]{2,1,0:T(2,128)(2,1)} %reshape.465), calls=%async_computation.1 | async-start | bytes 3981312 | tf_op jit(solution)/shard_map/all_to_all | solution.py:77
  520.5 113.9 %copy-start.1 = (bf16[288,384]{1,0:T(8,128)(2,1)S(1)}, bf16[288,384]{1,0:T(8,128)(2,1)}, u32[]{:S(2)}) copy-start(bf16[288,384]{1,0:T(8,128)(2,1)} %param.6) | copy-start | bytes 663556
  603.9 27.8 %collective-permute-start = (bf16[96,384]{1,0:T(8,128)(2,1)S(1)}, bf16[96,384]{1,0:T(8,128)(2,1)S(1)}, u32[]{:S(2)}, u32[]{:S(2)}) collective-permute-start(bf16[96,384]{1,0:T(8,128)(2,1)S(1)} %fusion), channel_id=1, source_target_pairs={{0,1},{1,2},{2,3},{3,4},{4,5},{5,6},{6,7},{7,8},{8,9},{9,10},{10,1... | collective-permute-start | bytes 221192
  607.5 24.3 %collective-permute-start.1 = (bf16[96,384]{1,0:T(8,128)(2,1)S(1)}, bf16[96,384]{1,0:T(8,128)(2,1)S(1)}, u32[]{:S(2)}, u32[]{:S(2)}) collective-permute-start(bf16[96,384]{1,0:T(8,128)(2,1)S(1)} %fusion), channel_id=1, source_target_pairs={{0,2},{1,3},{2,4},{3,5},{4,6},{5,7},{6,8},{7,9},{8,10},{9,11},{10,... | collective-permute-start | bytes 221192
  608.8 23.0 %collective-permute-start.2 = (bf16[96,384]{1,0:T(8,128)(2,1)S(1)}, bf16[96,384]{1,0:T(8,128)(2,1)S(1)}, u32[]{:S(2)}, u32[]{:S(2)}) collective-permute-start(bf16[96,384]{1,0:T(8,128)(2,1)S(1)} %fusion), channel_id=1, source_target_pairs={{0,3},{1,4},{2,5},{3,6},{4,7},{5,8},{6,9},{7,10},{8,11},{9,12},{10... | collective-permute-start | bytes 221192
  610.1 21.7 %collective-permute-start.3 = (bf16[96,384]{1,0:T(8,128)(2,1)S(1)}, bf16[96,384]{1,0:T(8,128)(2,1)S(1)}, u32[]{:S(2)}, u32[]{:S(2)}) collective-permute-start(bf16[96,384]{1,0:T(8,128)(2,1)S(1)} %fusion), channel_id=1, source_target_pairs={{0,4},{1,5},{2,6},{3,7},{4,8},{5,9},{6,10},{7,11},{8,12},{9,13},{1... | collective-permute-start | bytes 221192
  611.4 20.3 %collective-permute-start.4 = (bf16[81,384]{1,0:T(8,128)(2,1)S(1)}, bf16[81,384]{1,0:T(8,128)(2,1)S(1)}, u32[]{:S(2)}, u32[]{:S(2)}) collective-permute-start(bf16[81,384]{1,0:T(8,128)(2,1)S(1)} %slice.16), channel_id=1, source_target_pairs={{0,5},{1,6},{2,7},{3,8},{4,9},{5,10},{6,11},{7,12},{8,13},{9,14},{... | collective-permute-start | bytes 186632
Sparse Core Ops, SparseCore 0:
  13.4 98.1 all-gather.5
  113.7 100.7 all-gather.7
  216.6 82.7 all-gather.9
  301.3 83.2 all-gather.11
where the time goes:
time: 642 us; the launch traced here: 641 us
  waiting for transfers between devices  292 us (45%)
  blocking collectives  154 us (24%)
  local copies, waits for them, and re-layouts  85.7 us (13%)
  other arithmetic  56.5 us (9%)
  starting transfers between devices  28.5 us (4%)
  between operations  14.1 us (2%)
  matrix products  10.2 us (2%)
    all_gather x1, waiting for transfers between devices, local(): selected = lax.all_gather(own_slots, 'ed', axis=1, tiled=True)  96.3 us
    all_gather x1, waiting for transfers between devices, local(): lax.all_gather(w_down[0], 'fsdp', axis=1, tiled=True)  85.3 us
    unnamed x1, blocking collectives  81.8 us
    all_to_all x1, blocking collectives, local(): lax.all_to_all(selected, 'fsdp', split_axis=1, concat_axis=2, tiled=True)  71.7 us
    all_gather x1, waiting for transfers between devices, local(): lax.all_gather(w_up, 'fsdp', axis=1, tiled=True)  66.1 us
    unnamed x2, other arithmetic  50.5 us
    all_to_all x1, waiting for transfers between devices, local(): lax.all_to_all(stacked, 'fsdp', split_axis=2, concat_axis=1, tiled=True)  42.9 us
    unnamed x19, local copies, waits for them, and re-layouts  34.1 us
  transfers between devices with their start and end apart: 10, of which 4 were waited for; matrix products, arithmetic and copies ran while one was open for 8% of the time, Pallas kernels for 0%

commit v1 on v0

--- a/solution.py
+++ b/solution.py
@@ -51,7 +51,9 @@
     window = w_gate.shape[0]
     features_dev = tokens.shape[1]
     own_slots = pick_rows(tokens[None], expert_ids[None], window, CAP)[0]
-    selected = lax.all_gather(own_slots, "ed", axis=1, tiled=True)
+    selected = jnp.concatenate(
+        lax.all_to_all(jnp.stack([own_slots] * lax.axis_size("ed")), "ed", 0, 0), axis=1
+    )
     rows_full = lax.all_to_all(selected, "fsdp", split_axis=1, concat_axis=2, tiled=True)
     gate_part = jnp.einsum(
         "hnm,hmq->hnq",

time: 642 us -> 562 us (0.88)
  waiting for transfers between devices: 292 us -> 202 us
  starting transfers between devices: 28.5 us -> 42.9 us
  blocking collectives: 154 us -> 140 us
  local copies, waits for them, and re-layouts: 85.7 us -> 94.4 us
    all_gather x1 -> x0, waiting for transfers between devices: 96.3 us -> none  [local(): selected = lax.all_gather(own_slots, 'ed', axis=1, tiled=True)]
    all_to_all x0 -> x1, waiting for transfers between devices: none -> 51.1 us  [local(): lax.all_to_all(jnp.stack([own_slots] * lax.axis_size('ed')), 'ed', 0, 0)]
    all_gather x1, waiting for transfers between devices: 66.1 us -> 21.7 us  [local(): lax.all_gather(w_up, 'fsdp', axis=1, tiled=True)]
    all_to_all x0 -> x1, starting transfers between devices: none -> 14.4 us  [local(): lax.all_to_all(jnp.stack([own_slots] * lax.axis_size('ed')), 'ed', 0, 0)]
    all_to_all x1, blocking collectives: 71.7 us -> 58.5 us  [local(): lax.all_to_all(selected, 'fsdp', split_axis=1, concat_axis=2, tiled=True)]
    reshape x0 -> x1, local copies, waits for them, and re-layouts: none -> 7.92 us  [local(): jnp.concatenate(lax.all_to_all(jnp.stack([own_slots] * lax.axis_size('ed'...]
  transfers between devices with their start and end apart: 10 -> 10, of which waited for: 4 -> 4; matrix products, arithmetic and copies ran while one was open for 8% -> 12% of each run, Pallas kernels for 0% -> 0%
where the time goes in v1:
time: 562 us; the launch traced here: 561 us
  waiting for transfers between devices  202 us (36%)
  blocking collectives  140 us (25%)
  local copies, waits for them, and re-layouts  94.4 us (17%)
  other arithmetic  56.5 us (10%)
  starting transfers between devices  42.9 us (8%)
  between operations  14 us (2%)
  matrix products  10.4 us (2%)
    all_gather x1, waiting for transfers between devices, local(): lax.all_gather(w_down[0], 'fsdp', axis=1, tiled=True)  84.3 us
    unnamed x1, blocking collectives  81.8 us
    all_to_all x1, blocking collectives, local(): lax.all_to_all(selected, 'fsdp', split_axis=1, concat_axis=2, tiled=True)  58.5 us
    all_to_all x1, waiting for transfers between devices, local(): lax.all_to_all(jnp.stack([own_slots] * lax.axis_size('ed')), 'ed', 0, 0)  51.1 us
    unnamed x2, other arithmetic  50.5 us
    all_to_all x1, waiting for transfers between devices, local(): lax.all_to_all(stacked, 'fsdp', split_axis=2, concat_axis=1, tiled=True)  42.9 us
    unnamed x19, local copies, waits for them, and re-layouts  34.1 us
    unnamed x5, starting transfers between devices  24.1 us
  transfers between devices with their start and end apart: 10, of which 4 were waited for; matrix products, arithmetic and copies ran while one was open for 12% of the time, Pallas kernels for 0%

profile of v1, /device:TPU:1, one launch (start us, length us, event | category | flops | bytes accessed | tf_op | source)
XLA Modules:
  0.0 560.6 jit_solution(11562746356790680400)
XLA Ops:
  6.5 0.0 copy-start
  6.5 0.0 all-gather.5.cloned.1.call-start
  6.5 0.7 all-gather.5.cloned.1.call-update
  7.3 0.0 all-gather.7.cloned.1.call-start
  7.3 0.7 all-gather.7.cloned.1.call-update
  8.0 0.7 fusion.26
  8.7 0.3 reduce-window.6
  9.1 0.2 slice_reduce_fusion
  9.3 0.2 reduce-window.9
  9.4 0.1 broadcast.242
  9.6 3.0 convert_reduce_fusion
  12.6 0.0 copy-done
  12.6 1.3 gather_fusion
  13.9 0.1 select_select_fusion
  14.0 1.5 stack.6
  15.5 14.4 %all-to-all-start = ((bf16[32,1,81,384]{3,2,1,0:T(8,128)(2,1)}), bf16[32,1,81,384]{3,2,1,0:T(8,128)(2,1)S(1)}, u32[]{:S(2)}, u32[]{:S(2)}) async-start(bf16[32,1,81,384]{3,2,1,0:T(8,128)(2,1)} %stack.6), calls=%async_computation | async-start | bytes 4325376 | tf_op jit(solution)/shard_map/all_to_all | solution.py:55
  30.0 0.0 all-gather.9.cloned.1.call-start
  30.0 0.7 all-gather.9.cloned.1.call-update
  30.7 51.1 %all-to-all-done = bf16[32,1,81,384]{3,2,1,0:T(8,128)(2,1)S(1)} async-done(((bf16[32,1,81,384]{3,2,1,0:T(8,128)(2,1)}), bf16[32,1,81,384]{3,2,1,0:T(8,128)(2,1)S(1)}, u32[]{:S(2)}, u32[]{:S(2)}) %all-to-all-start) | async-done | bytes 1990688 | tf_op jit(solution)/shard_map/all_to_all | solution.py:55
  81.8 7.9 %reshape.449 = bf16[1,2592,384]{2,0,1:T(2,128)(2,1)} reshape(bf16[32,1,81,384]{3,2,1,0:T(8,128)(2,1)S(1)} %all-to-all-done) | data formatting | bytes 3981312 | tf_op jit(solution)/shard_map/reshape | solution.py:54
  89.7 0.5 broadcast.267
  90.2 15.8 %reduce.14 = bf16[2592,384]{1,0:T(8,128)(2,1)S(1)} reduce(bf16[2592,1,384]{2,1,0:T(2,128)(2,1)} %bitcast.71, bf16[]{:T(256)} %broadcast.267), dimensions={1}, to_apply=%bitcast.57.reduce_sub_computation | reduce | bytes 3981314
  106.1 1.6 reshape.457
  107.7 58.5 %all_to_all.38 = bf16[16,2,31104]{2,1,0:T(2,128)(2,1)S(1)} all-to-all(bf16[16,2,31104]{2,1,0:T(2,128)(2,1)} %reshape.457), channel_id=1, replica_groups=mesh['fsdp'=16,'ed'=32] {'fsdp'}, dimensions={0} | all-to-all | bytes 3981312 | tf_op jit(solution)/shard_map/all_to_all | solution.py:57
  166.1 8.9 %reshape.458 = bf16[2592,1,384]{2,1,0:T(2,128)(2,1)} reshape(bf16[16,2,31104]{2,1,0:T(2,128)(2,1)S(1)} %all_to_all.38) | data formatting | bytes 3981312
  175.0 17.6 %bitcast_reduce_fusion = bf16[2592,384]{1,0:T(8,128)(2,1)} fusion(bf16[2592,1,384]{2,1,0:T(2,128)(2,1)} %reshape.458), kind=kLoop, calls=%fused_computation.45 | loop fusion | bytes 3981312 | tf_op jit(solution)/shard_map/all_to_all | solution.py:57
  192.6 1.8 all_to_all.29
  194.4 0.3 copy.29
  194.7 0.2 pad.7
  194.9 0.5 copy.26
  195.4 0.0 all-gather.5.cloned.1.call-done
  195.5 2.7 fusion.5
  198.2 21.7 %all-gather.7.cloned.1.call-done = bf16[1,6144,256]{2,1,0:T(8,128)(2,1)} async-done(((bf16[1,384,256]{2,1,0:T(8,128)(2,1)}), bf16[1,6144,256]{2,1,0:T(8,128)(2,1)}) %all-gather.7.cloned.1.call-update) | async-done | bytes 3145744 | tf_op jit(solution)/shard_map/all_gather | solution.py:67
  219.9 84.3 %all-gather.9.cloned.1.call-done = bf16[1,256,6144]{2,1,0:T(8,128)(2,1)} async-done(((bf16[1,256,384]{2,1,0:T(8,128)(2,1)}), bf16[1,256,6144]{2,1,0:T(8,128)(2,1)}) %all-gather.9.cloned.1.call-update) | async-done | bytes 3145744 | tf_op jit(solution)/shard_map/all_gather | solution.py:76
  304.2 6.6 %fusion.1 = bf16[1,162,6144]{2,1,0:T(8,128)(2,1)} fusion(bf16[1,256,6144]{2,1,0:T(8,128)(2,1)} %all-gather.9.cloned.1.call-done, bf16[162,6144]{1,0:T(8,128)(2,1)S(1)} %bitcast.70, bf16[1,6144,256]{2,1,0:T(8,128)(2,1)} %all-gather.7.cloned.1.call-done, f32[162,256]{1,0:T(8,128)S(1)} %fusion.5), kind=kOutput, calls=%fused_computation.2 | convolution fusion | flops 1020460032 | bytes 10438656 | tf_op jit(solution)/shard_map/dot_general | solution.py:74
  310.9 13.7 %copy.20 = bf16[1,162,6144]{1,0,2:T(2,128)(2,1)} copy(bf16[1,162,6144]{2,1,0:T(8,128)(2,1)} %fusion.1) | data formatting | bytes 3981312 | tf_op jit(solution)/shard_map/stack | solution.py:78
  324.6 34.6 %reduce.15 = bf16[6144,162]{1,0:T(8,128)(2,1)S(1)} reduce(bf16[6144,1,162]{2,1,0:T(2,128)(2,1)} %bitcast.67, bf16[]{:T(256)} %broadcast.267), dimensions={1}, to_apply=%bitcast.59.reduce_sub_computation | reduce | bytes 3981314
  359.2 6.9 %reshape.459 = bf16[16,2,31104]{2,1,0:T(2,128)(2,1)} reshape(bf16[6144,162]{1,0:T(8,128)(2,1)S(1)} %reduce.15) | data formatting | bytes 3981312
  366.1 4.2 all-to-all-start.2
  370.3 0.0 copy-done.2
  370.3 0.0 copy-done.3
  370.4 42.9 %all-to-all-done.2 = bf16[16,2,31104]{2,1,0:T(2,128)(2,1)S(1)} async-done(((bf16[16,2,31104]{2,1,0:T(2,128)(2,1)}), bf16[16,2,31104]{2,1,0:T(2,128)(2,1)S(1)}, u32[]{:S(2)}, u32[]{:S(2)}) %all-to-all-start.2) | async-done | bytes 1990688 | tf_op jit(solution)/shard_map/all_to_all | solution.py:79
  413.2 12.1 %reshape.460 = bf16[6144,1,162]{2,1,0:T(2,128)(2,1)} reshape(bf16[16,2,31104]{2,1,0:T(2,128)(2,1)S(1)} %all-to-all-done.2) | data formatting | bytes 3981312
  425.3 13.8 %copy.21 = bf16[1,162,6144]{2,1,0:T(8,128)(2,1)S(1)} copy(bf16[1,162,6144]{1,0,2:T(2,128)(2,1)} %bitcast.68) | data formatting | bytes 3981312 | tf_op jit(solution)/shard_map/all_to_all | solution.py:79
  439.1 0.4 copy.27
  439.5 0.2 bitcast_bitcast_fusion
  439.7 0.4 copy.22
  440.2 0.0 copy-start.1
  440.2 1.6 all_to_all.34
  441.7 81.8 %fusion = bf16[96,384]{1,0:T(8,128)(2,1)S(1)} fusion(bf16[1,2592,384]{2,1,0:T(8,128)(2,1)} %all_to_all.34), kind=kCustom, calls=%all-reduce-scatter | all-reduce-scatter fusion | flops 1179649 | bytes 2066432
  523.6 3.5 collective-permute-start
  527.2 1.3 collective-permute-start.1
  528.5 1.3 collective-permute-start.2
  529.8 1.3 collective-permute-start.3
  531.1 16.7 %collective-permute-start.4 = (bf16[81,384]{1,0:T(8,128)(2,1)S(1)}, bf16[81,384]{1,0:T(8,128)(2,1)S(1)}, u32[]{:S(2)}, u32[]{:S(2)}) collective-permute-start(bf16[81,384]{1,0:T(8,128)(2,1)S(1)} %slice.16), channel_id=1, source_target_pairs={{0,5},{1,6},{2,7},{3,8},{4,9},{5,10},{6,11},{7,12},{8,13},{9,14},{... | collective-permute-start | bytes 186632
  547.8 1.7 convert_multiply_fusion
  549.5 1.3 dynamic-slice.4
  551.4 0.0 collective-permute-done.4
  551.4 0.0 collective-permute-done
  551.4 0.0 collective-permute-done.1
  551.5 0.0 collective-permute-done.2
  551.5 0.0 collective-permute-done.3
  551.5 1.6 concatenate.3
  553.1 1.0 convolution_convert_fusion.1
  (15 shorter events, 0.2 us)
Async XLA Ops:
  6.5 6.0 %copy-start = (bf16[288,384]{1,0:T(8,128)(2,1)S(1)}, bf16[288,384]{1,0:T(8,128)(2,1)}, u32[]{:S(2)}) copy-start(bf16[288,384]{1,0:T(8,128)(2,1)} %param.6) | copy-start | bytes 663556
  6.5 188.9 %all-gather.5.cloned.1.call-start = ((), (), s32[]{:S(2)}) async-start(), calls=%async_computation.3 | async-start | bytes 3342336 | tf_op jit(solution)/shard_map/all_gather | solution.py:61
  7.3 212.7 %all-gather.7.cloned.1.call-start = ((), (), s32[]{:S(2)}) async-start(), calls=%async_computation.4 | async-start | bytes 3342336 | tf_op jit(solution)/shard_map/all_gather | solution.py:67
  15.5 66.3 %all-to-all-start = ((bf16[32,1,81,384]{3,2,1,0:T(8,128)(2,1)}), bf16[32,1,81,384]{3,2,1,0:T(8,128)(2,1)S(1)}, u32[]{:S(2)}, u32[]{:S(2)}) async-start(bf16[32,1,81,384]{3,2,1,0:T(8,128)(2,1)} %stack.6), calls=%async_computation | async-start | bytes 4325376 | tf_op jit(solution)/shard_map/all_to_all | solution.py:55
  30.0 274.3 %all-gather.9.cloned.1.call-start = ((), (), s32[]{:S(2)}) async-start(), calls=%async_computation.5 | async-start | bytes 3342336 | tf_op jit(solution)/shard_map/all_gather | solution.py:76
  366.1 4.2 copy-start.2
  366.1 4.3 copy-start.3
  366.1 47.1 %all-to-all-start.2 = ((bf16[16,2,31104]{2,1,0:T(2,128)(2,1)}), bf16[16,2,31104]{2,1,0:T(2,128)(2,1)S(1)}, u32[]{:S(2)}, u32[]{:S(2)}) async-start(bf16[16,2,31104]{2,1,0:T(2,128)(2,1)} %reshape.459), calls=%async_computation.2 | async-start | bytes 3981312 | tf_op jit(solution)/shard_map/all_to_all | solution.py:79
  440.2 113.9 %copy-start.1 = (bf16[288,384]{1,0:T(8,128)(2,1)S(1)}, bf16[288,384]{1,0:T(8,128)(2,1)}, u32[]{:S(2)}) copy-start(bf16[288,384]{1,0:T(8,128)(2,1)} %param.6) | copy-start | bytes 663556
  523.6 27.8 %collective-permute-start = (bf16[96,384]{1,0:T(8,128)(2,1)S(1)}, bf16[96,384]{1,0:T(8,128)(2,1)S(1)}, u32[]{:S(2)}, u32[]{:S(2)}) collective-permute-start(bf16[96,384]{1,0:T(8,128)(2,1)S(1)} %fusion), channel_id=1, source_target_pairs={{0,1},{1,2},{2,3},{3,4},{4,5},{5,6},{6,7},{7,8},{8,9},{9,10},{10,1... | collective-permute-start | bytes 221192
  527.2 24.3 %collective-permute-start.1 = (bf16[96,384]{1,0:T(8,128)(2,1)S(1)}, bf16[96,384]{1,0:T(8,128)(2,1)S(1)}, u32[]{:S(2)}, u32[]{:S(2)}) collective-permute-start(bf16[96,384]{1,0:T(8,128)(2,1)S(1)} %fusion), channel_id=1, source_target_pairs={{0,2},{1,3},{2,4},{3,5},{4,6},{5,7},{6,8},{7,9},{8,10},{9,11},{10,... | collective-permute-start | bytes 221192
  528.5 23.0 %collective-permute-start.2 = (bf16[96,384]{1,0:T(8,128)(2,1)S(1)}, bf16[96,384]{1,0:T(8,128)(2,1)S(1)}, u32[]{:S(2)}, u32[]{:S(2)}) collective-permute-start(bf16[96,384]{1,0:T(8,128)(2,1)S(1)} %fusion), channel_id=1, source_target_pairs={{0,3},{1,4},{2,5},{3,6},{4,7},{5,8},{6,9},{7,10},{8,11},{9,12},{10... | collective-permute-start | bytes 221192
  529.8 21.7 %collective-permute-start.3 = (bf16[96,384]{1,0:T(8,128)(2,1)S(1)}, bf16[96,384]{1,0:T(8,128)(2,1)S(1)}, u32[]{:S(2)}, u32[]{:S(2)}) collective-permute-start(bf16[96,384]{1,0:T(8,128)(2,1)S(1)} %fusion), channel_id=1, source_target_pairs={{0,4},{1,5},{2,6},{3,7},{4,8},{5,9},{6,10},{7,11},{8,12},{9,13},{1... | collective-permute-start | bytes 221192
  531.1 20.3 %collective-permute-start.4 = (bf16[81,384]{1,0:T(8,128)(2,1)S(1)}, bf16[81,384]{1,0:T(8,128)(2,1)S(1)}, u32[]{:S(2)}, u32[]{:S(2)}) collective-permute-start(bf16[81,384]{1,0:T(8,128)(2,1)S(1)} %slice.16), channel_id=1, source_target_pairs={{0,5},{1,6},{2,7},{3,8},{4,9},{5,10},{6,11},{7,12},{8,13},{9,14},{... | collective-permute-start | bytes 186632
Sparse Core Ops, SparseCore 0:
  9.4 114.7 all-gather.4
  126.3 93.6 all-gather.6
  222.0 82.1 all-gather.8
